TPU v7x, 32 devices: a whole 2x2x4 slice. The times are simulated.
32 devices in a mesh: seq: 8 (over z, x), batch: 4 (over y, core).
Axes of the slice: x: 2, y: 2, z: 4, core: 2. Of those that a mesh axis runs over, the one named last changes fastest.
Arguments:
- tokens: bfloat16 [4, 2048, 2048], P('batch', 'seq'), may hold values from -6 to 6
- lengths: int32 [4, 1], replicated, may hold values from 512 to 2048, as said below
- cotangent: bfloat16 [4, 2048, 2048], P('batch', 'seq'), may hold values from -6 to 6
- ln1_gain: bfloat16 [2048], P(('seq', 'batch')), may hold values from 0.5 to 1.5
- ln1_bias: bfloat16 [2048], P(('seq', 'batch')), may hold values from -1.5 to 1.5
- w_qkv: bfloat16 [2048, 3, 2048], P('seq', None, 'batch'), may hold values from -0.1875 to 0.1875
- qv_bias: bfloat16 [2, 2048], P(None, 'batch'), may hold values from -1.5 to 1.5
- w_out: bfloat16 [2048, 2048], P('batch', 'seq'), may hold values from -0.375 to 0.375
- out_bias: bfloat16 [2048], P(('seq', 'batch')), may hold values from -1.5 to 1.5
- ln2_gain: bfloat16 [2048], P(('seq', 'batch')), may hold values from 0.5 to 1.5
- ln2_bias: bfloat16 [2048], P(('seq', 'batch')), may hold values from -1.5 to 1.5
- w_fc: bfloat16 [2048, 8192], P('seq', 'batch'), may hold values from -0.125 to 0.125
- fc_bias: bfloat16 [8192], P('batch'), may hold values from -1.5 to 1.5
- w_proj: bfloat16 [8192, 2048], P('batch', 'seq'), may hold values from -0.0625 to 0.0625
- proj_bias: bfloat16 [2048], P(('seq', 'batch')), may hold values from -1.5 to 1.5
Outputs:
- block_out: bfloat16 [4, 2048, 2048], P('batch', 'seq')
- grad_tokens: bfloat16 [4, 2048, 2048], P('batch', 'seq')
- grad_ln1_gain: float32 [2048], P(('seq', 'batch'))
- grad_ln1_bias: float32 [2048], P(('seq', 'batch'))
- grad_w_qkv: float32 [2048, 3, 2048], P('seq', None, 'batch')
- grad_qv_bias: float32 [2, 2048], P(None, 'batch')
- grad_w_out: float32 [2048, 2048], P('batch', 'seq')
- grad_out_bias: float32 [2048], P(('seq', 'batch'))
- grad_ln2_gain: float32 [2048], P(('seq', 'batch'))
- grad_ln2_bias: float32 [2048], P(('seq', 'batch'))
- grad_w_fc: float32 [2048, 8192], P('seq', 'batch')
- grad_fc_bias: float32 [8192], P('batch')
- grad_w_proj: float32 [8192, 2048], P('batch', 'seq')
- grad_proj_bias: float32 [2048], P(('seq', 'batch'))
Inputs may be any that keep to these rules, and one draw needn't show every extreme that they name: `lengths`: some sequence has all 2048 slots true and some other has exactly 512.
All inputs are finite; a program needn't handle non-finite values.
Results may differ from a plain program's by a relative error of at most 0.018.
Values may be sent and summed in bfloat16 or wider, within the bound.
No kernel may reach another device: no remote copies, remote signals or barrier semaphores. Data moves between devices by JAX's collectives and lax.ppermute only.
A program may use at most 448 MiB of HBM per device.

v0:
```python
import jax
import jax.numpy as jnp
from jax import lax
from jax.sharding import PartitionSpec as P

HEAD_DIM = 128
WINDOW = 256


def shifted(value, axis, steps):
    count = lax.axis_size(axis)
    initial, last = (max(0, -steps), min(count, count - steps))
    return lax.ppermute(value, axis, [(source, source + steps) for source in range(initial, last)])


def layer_norm(values, gain, shift):
    mean = jnp.mean(values, axis=-1, keepdims=True)
    centered = values - mean
    factor = lax.rsqrt(jnp.mean(centered * centered, axis=-1, keepdims=True) + 1e-05)
    return centered * factor * gain + shift


def gelu_tanh(values):
    return jax.nn.gelu(values, approximate=True)


def allowed_keys(query_pos, key_pos, limit, seq_length):
    later = query_pos[:, None]
    earlier = key_pos[None, :]
    gap = later - earlier
    same = later // seq_length == earlier // seq_length
    live = (earlier % seq_length < limit[:, None]) | (gap == 0)
    return (earlier >= 0) & (gap >= 0) & (gap < WINDOW) & same & live


def limits_of(chain_lengths, chain_pos, seq_length):
    owner = chain_pos // seq_length
    slots = jnp.arange(chain_lengths.shape[1], dtype=jnp.int32)
    match = owner[:, None] == slots[None, :]
    return jnp.sum(jnp.where(match[None], chain_lengths[:, None, :], 0), axis=2)


def bias_total(values):
    return lax.psum(values.astype(jnp.bfloat16), "seq").astype(jnp.float32)


def rows_total(pair):
    return (
        lax.psum_scatter(
            pair[0].astype(jnp.bfloat16), "seq", scatter_dimension=0, tiled=True
        ).astype(jnp.float32),
        lax.psum_scatter(
            pair[1].astype(jnp.bfloat16), "seq", scatter_dimension=1, tiled=True
        ).astype(jnp.float32),
    )


def shards(
    tokens,
    lengths,
    cotangent,
    ln1_gain,
    ln1_bias,
    w_qkv,
    qv_bias,
    w_out,
    out_bias,
    ln2_gain,
    ln2_bias,
    w_fc,
    fc_bias,
    w_proj,
    proj_bias,
):
    floaty = jnp.float32
    brain = jnp.bfloat16
    rows = tokens.shape[1]
    width = tokens.shape[2]
    head_dim = HEAD_DIM
    scale = head_dim ** (-0.5)
    seq_length = rows * lax.axis_size("seq") // lengths.shape[1]
    norm_vectors = (
        lax.all_gather(ln1_gain, ("seq", "batch"), axis=0, tiled=True),
        lax.all_gather(ln1_bias, ("seq", "batch"), axis=0, tiled=True),
        lax.all_gather(out_bias, ("seq", "batch"), axis=0, tiled=True),
        lax.all_gather(ln2_gain, ("seq", "batch"), axis=0, tiled=True),
        lax.all_gather(ln2_bias, ("seq", "batch"), axis=0, tiled=True),
        lax.all_gather(proj_bias, ("seq", "batch"), axis=0, tiled=True),
    )
    gain_one, shift_one, mix_shift, gain_two, shift_two, down_shift = (
        v.astype(floaty) for v in norm_vectors
    )
    proj_in, proj_mix, proj_up, proj_down = (
        lax.all_gather(w_qkv, "seq", axis=0, tiled=True),
        lax.all_gather(w_out, "seq", axis=1, tiled=True),
        lax.all_gather(w_fc, "seq", axis=0, tiled=True),
        lax.all_gather(w_proj, "seq", axis=1, tiled=True),
    )
    own_lengths = lax.dynamic_slice_in_dim(lengths, lax.axis_index("batch"), 1, 0)
    proj_in, qv_shift, proj_mix, proj_up, up_shift, proj_down = (
        lax.all_gather(proj_in, "batch", axis=2, tiled=True),
        lax.all_gather(qv_bias, "batch", axis=1, tiled=True),
        lax.all_gather(proj_mix, "batch", axis=0, tiled=True),
        lax.all_gather(proj_up, "batch", axis=1, tiled=True),
        lax.all_gather(fc_bias, "batch", axis=0, tiled=True),
        lax.all_gather(proj_down, "batch", axis=0, tiled=True),
    )
    local_width = proj_in.shape[2]
    local_heads = local_width // head_dim
    chains = own_lengths.shape[0]
    flat_rows = chains * rows
    block_start = lax.axis_index("seq") * rows
    chain_pos = block_start + jnp.arange(rows, dtype=jnp.int32)
    key_pos = block_start - WINDOW + jnp.arange(rows + WINDOW, dtype=jnp.int32)
    own_limit = limits_of(own_lengths, chain_pos, seq_length)[0]
    valid = (chain_pos % seq_length < own_limit).astype(floaty)
    limits = limits_of(own_lengths, chain_pos, seq_length)
    mask = jax.vmap(lambda bound: allowed_keys(chain_pos, key_pos, bound, seq_length))(limits)
    inputs = tokens.astype(floaty)
    normed_f, norm_one_back = jax.vjp(layer_norm, inputs, gain_one, shift_one)
    normed = normed_f.astype(brain).reshape(flat_rows, width)
    packed = jnp.dot(
        normed, proj_in.reshape(width, 3 * local_width), preferred_element_type=floaty
    ).reshape(chains, rows, 3, local_width)
    qv_float = qv_shift.astype(floaty)
    query = (packed[:, :, 0] + qv_float[0]).astype(brain)
    key = packed[:, :, 1].astype(brain)
    value = (packed[:, :, 2] + qv_float[1]).astype(brain)
    halo_keys, halo_values = shifted((key, value), "seq", 1)
    keys = jnp.concatenate([halo_keys, key], axis=1).reshape(
        chains, rows + WINDOW, local_heads, head_dim
    )
    values = jnp.concatenate([halo_values, value], axis=1).reshape(
        chains, rows + WINDOW, local_heads, head_dim
    )
    query4 = query.reshape(chains, rows, local_heads, head_dim)
    scores = jnp.einsum("cqhd,ckhd->chqk", query4, keys, preferred_element_type=floaty) * scale
    scores = jnp.where(mask[:, None], scores, -1e30)
    top = jnp.max(scores, axis=-1, keepdims=True)
    expo = jnp.exp(scores - top)
    total = jnp.sum(expo, axis=-1, keepdims=True)
    logsum = top + jnp.log(total)
    probs = (expo / total).astype(brain)
    mixed = (
        jnp.einsum("chqk,ckhd->cqhd", probs, values, preferred_element_type=floaty)
        .reshape(flat_rows, local_width)
        .astype(brain)
    )
    branch = jnp.dot(mixed, proj_mix, preferred_element_type=floaty).reshape(chains, rows, width)
    resid = inputs + branch + mix_shift
    second_f, norm_two_back = jax.vjp(layer_norm, resid, gain_two, shift_two)
    second = second_f.astype(brain).reshape(flat_rows, width)
    pre = jnp.dot(second, proj_up, preferred_element_type=floaty) + up_shift.astype(floaty)
    active_f, gelu_back = jax.vjp(gelu_tanh, pre)
    active = active_f.astype(brain)
    ffn = jnp.dot(active, proj_down, preferred_element_type=floaty).reshape(chains, rows, width)
    result = resid + ffn + down_shift
    block_out = result.astype(brain)
    grad_out = cotangent.astype(floaty) * valid[None, :, None]
    grad_y_own = grad_out.astype(brain)
    grad_proj_bias = jnp.sum(grad_y_own.astype(floaty), axis=(0, 1))
    grad_y = grad_y_own.reshape(flat_rows, width)
    grad_w_proj = jnp.einsum("tf,td->fd", active, grad_y, preferred_element_type=floaty)
    grad_active = jnp.einsum("td,fd->tf", grad_y, proj_down, preferred_element_type=floaty)
    grad_pre = gelu_back(grad_active)[0].astype(brain)
    grad_fc_bias = bias_total(jnp.sum(grad_pre.astype(floaty), axis=0))
    grad_w_fc = jnp.einsum("td,tf->df", second, grad_pre, preferred_element_type=floaty)
    grad_second = jnp.einsum("tf,df->td", grad_pre, proj_up, preferred_element_type=floaty).reshape(
        chains, rows, width
    )
    grad_resid_norm, grad_ln2_gain, grad_ln2_bias = norm_two_back(grad_second)
    grad_resid = grad_out + grad_resid_norm
    fc_rows, proj_rows = rows_total((grad_w_fc, grad_w_proj))
    fc_rows, grad_fc_bias, proj_rows = (
        lax.psum_scatter(
            fc_rows.astype(jnp.bfloat16), "batch", scatter_dimension=1, tiled=True
        ).astype(jnp.float32),
        lax.psum_scatter(
            grad_fc_bias.astype(jnp.bfloat16), "batch", scatter_dimension=0, tiled=True
        ).astype(jnp.float32),
        lax.psum_scatter(
            proj_rows.astype(jnp.bfloat16), "batch", scatter_dimension=0, tiled=True
        ).astype(jnp.float32),
    )
    grad_branch_own = grad_resid.astype(brain)
    grad_out_bias = jnp.sum(grad_branch_own.astype(floaty), axis=(0, 1))
    grad_branch = grad_branch_own.reshape(flat_rows, width)
    grad_w_out = jnp.einsum("td,te->de", mixed, grad_branch, preferred_element_type=floaty)
    grad_mixed = jnp.einsum(
        "te,de->td", grad_branch, proj_mix, preferred_element_type=floaty
    ).astype(brain)
    grad_mixed4 = grad_mixed.reshape(chains, rows, local_heads, head_dim)
    again = jnp.einsum("cqhd,ckhd->chqk", query4, keys, preferred_element_type=floaty) * scale
    weights_f = jnp.where(mask[:, None], jnp.exp(again - logsum), 0.0)
    grad_probs = jnp.einsum("cqhd,ckhd->chqk", grad_mixed4, values, preferred_element_type=floaty)
    delta = jnp.sum(weights_f * grad_probs, axis=-1, keepdims=True)
    grad_scores = (weights_f * (grad_probs - delta)).astype(brain)
    grad_values = jnp.einsum(
        "chqk,cqhd->ckhd", weights_f.astype(brain), grad_mixed4, preferred_element_type=floaty
    ).reshape(chains, rows + WINDOW, local_width)
    grad_query = (
        (jnp.einsum("chqk,ckhd->cqhd", grad_scores, keys, preferred_element_type=floaty) * scale)
        .reshape(chains, rows, local_width)
        .astype(brain)
    )
    grad_keys = (
        jnp.einsum("chqk,cqhd->ckhd", grad_scores, query4, preferred_element_type=floaty) * scale
    ).reshape(chains, rows + WINDOW, local_width)
    back_keys, back_values = (
        shifted(grad_keys[:, :WINDOW].astype(jnp.bfloat16), "seq", -1).astype(jnp.float32),
        shifted(grad_values[:, :WINDOW].astype(jnp.bfloat16), "seq", -1).astype(jnp.float32),
    )
    own_keys = grad_keys[:, WINDOW:]
    own_values = grad_values[:, WINDOW:]
    own_keys = jnp.concatenate([own_keys[:, : rows - WINDOW], own_keys + back_keys], axis=1).astype(
        brain
    )
    own_values = jnp.concatenate(
        [own_values[:, : rows - WINDOW], own_values + back_values], axis=1
    ).astype(brain)
    grad_packed = jnp.stack([grad_query, own_keys, own_values], axis=2).reshape(
        flat_rows, 3 * local_width
    )
    grad_qv_bias = bias_total(
        jnp.stack(
            [
                jnp.sum(grad_query.astype(floaty), axis=(0, 1)),
                jnp.sum(own_values.astype(floaty), axis=(0, 1)),
            ],
            axis=0,
        )
    )
    grad_w_qkv = jnp.einsum(
        "td,te->de", normed, grad_packed, preferred_element_type=floaty
    ).reshape(width, 3, local_width)
    grad_normed = jnp.einsum(
        "te,de->td",
        grad_packed,
        proj_in.reshape(width, 3 * local_width),
        preferred_element_type=floaty,
    ).reshape(chains, rows, width)
    grad_input_norm, grad_ln1_gain, grad_ln1_bias = norm_one_back(grad_normed)
    grad_tokens = (grad_resid + grad_input_norm).astype(brain)
    qkv_rows, out_rows = rows_total((grad_w_qkv, grad_w_out))
    qkv_rows, grad_qv_bias, out_rows = (
        lax.psum_scatter(
            qkv_rows.astype(jnp.bfloat16), "batch", scatter_dimension=2, tiled=True
        ).astype(jnp.float32),
        lax.psum_scatter(
            grad_qv_bias.astype(jnp.bfloat16), "batch", scatter_dimension=1, tiled=True
        ).astype(jnp.float32),
        lax.psum_scatter(
            out_rows.astype(jnp.bfloat16), "batch", scatter_dimension=0, tiled=True
        ).astype(jnp.float32),
    )
    norm_sums = (
        lax.psum_scatter(grad_ln1_gain, ("seq", "batch"), scatter_dimension=0, tiled=True),
        lax.psum_scatter(grad_ln1_bias, ("seq", "batch"), scatter_dimension=0, tiled=True),
        lax.psum_scatter(grad_out_bias, ("seq", "batch"), scatter_dimension=0, tiled=True),
        lax.psum_scatter(grad_ln2_gain, ("seq", "batch"), scatter_dimension=0, tiled=True),
        lax.psum_scatter(grad_ln2_bias, ("seq", "batch"), scatter_dimension=0, tiled=True),
        lax.psum_scatter(grad_proj_bias, ("seq", "batch"), scatter_dimension=0, tiled=True),
    )
    return (
        block_out,
        grad_tokens,
        norm_sums[0],
        norm_sums[1],
        qkv_rows,
        grad_qv_bias,
        out_rows,
        norm_sums[2],
        norm_sums[3],
        norm_sums[4],
        fc_rows,
        grad_fc_bias,
        proj_rows,
        norm_sums[5],
    )


def solution(mesh):
    placed = (
        P("batch", "seq", None),
        P(),
        P("batch", "seq", None),
        P(("seq", "batch")),
        P(("seq", "batch")),
        P("seq", None, "batch"),
        P(None, "batch"),
        P("batch", "seq"),
        P(("seq", "batch")),
        P(("seq", "batch")),
        P(("seq", "batch")),
        P("seq", "batch"),
        P("batch"),
        P("batch", "seq"),
        P(("seq", "batch")),
    )
    return jax.shard_map(
        shards,
        mesh=mesh,
        in_specs=placed,
        out_specs=(
            P("batch", "seq", None),
            P("batch", "seq", None),
            P(("seq", "batch")),
            P(("seq", "batch")),
            P("seq", None, "batch"),
            P(None, "batch"),
            P("batch", "seq"),
            P(("seq", "batch")),
            P(("seq", "batch")),
            P(("seq", "batch")),
            P("seq", "batch"),
            P("batch"),
            P("batch", "seq"),
            P(("seq", "batch")),
        ),
        check_vma=False,
    )
```

profile of v0, /device:TPU:0, one launch (start us, length us, event | category | flops | bytes accessed | tf_op | source)
XLA Modules:
  0.0 2975.8 jit_solution(15007568904424727592)
XLA Ops:
  11.7 101.7 %all-gather.9.cloned.1.call-done = bf16[2048,3,512]{0,2,1:T(8,128)(2,1)} async-done(((bf16[256,3,512]{0,2,1:T(8,128)(2,1)}), bf16[2048,3,512]{0,2,1:T(8,128)(2,1)}) %all-gather.9.cloned.1.call-update) | async-done | bytes 6291472 | tf_op jit(solution)/shard_map/all_gather | solution.py:94
  113.4 51.3 %all-gather.13.cloned.1.call-done = bf16[512,2048]{1,0:T(8,128)(2,1)} async-done(((bf16[512,256]{1,0:T(8,128)(2,1)}), bf16[512,2048]{1,0:T(8,128)(2,1)}) %all-gather.13.cloned.1.call-update) | async-done | bytes 2097168 | tf_op jit(solution)/shard_map/all_gather | solution.py:95
  164.7 125.2 %all-gather.17.cloned.1.call-done = bf16[2048,2048]{1,0:T(8,128)(2,1)} async-done(((bf16[256,2048]{1,0:T(8,128)(2,1)}), bf16[2048,2048]{1,0:T(8,128)(2,1)}) %all-gather.17.cloned.1.call-update) | async-done | bytes 8388624 | tf_op jit(solution)/shard_map/all_gather | solution.py:96
  290.0 125.4 %all-gather.21.cloned.1.call-done = bf16[2048,2048]{1,0:T(8,128)(2,1)} async-done(((bf16[2048,256]{1,0:T(8,128)(2,1)}), bf16[2048,2048]{1,0:T(8,128)(2,1)}) %all-gather.21.cloned.1.call-update) | async-done | bytes 8388624 | tf_op jit(solution)/shard_map/all_gather | solution.py:97
  417.5 39.1 %all-reduce.14 = (bf16[2048]{0:T(1024)(128)(2,1)S(1)}, bf16[2048]{0:T(1024)(128)(2,1)S(1)}, bf16[2048]{0:T(1024)(128)(2,1)S(1)}, bf16[2048]{0:T(1024)(128)(2,1)}...) all-reduce(bf16[2048]{0:T(1024)(128)(2,1)S(1)} %dynamic-update-slic, ...), channel_id=1, replica_groups=mesh['seq'=8,'batch'=4] {'seq','batch'}, use_global_device_ids=true, to_apply=%add.1 | all-reduce | flops 12288 | bytes 49152
  470.9 99.9 %all-gather.11.cloned.1.call-done = bf16[2048,3,2048]{0,2,1:T(8,128)(2,1)} async-done(((bf16[2048,3,512]{0,2,1:T(8,128)(2,1)}), bf16[2048,3,2048]{0,2,1:T(8,128)(2,1)}) %all-gather.11.cloned.1.call-update) | async-done | bytes 25165840 | tf_op jit(solution)/shard_map/all_gather | solution.py:101
  570.8 13.9 fusion.18
  617.3 19.5 collective-permute-done.1
  651.3 8.9 fusion.97
  660.6 173.1 %all-gather.19.cloned.1.call-done = bf16[2048,8192]{1,0:T(8,128)(2,1)} async-done(((bf16[2048,2048]{1,0:T(8,128)(2,1)}), bf16[2048,8192]{1,0:T(8,128)(2,1)}) %all-gather.19.cloned.1.call-update) | async-done | bytes 33554448 | tf_op jit(solution)/shard_map/all_gather | solution.py:104
  833.6 21.9 convolution_add_fusion
  855.5 181.2 %all-gather.23.cloned.1.call-done = bf16[8192,2048]{1,0:T(8,128)(2,1)} async-done(((bf16[2048,2048]{1,0:T(8,128)(2,1)}), bf16[8192,2048]{1,0:T(8,128)(2,1)}) %all-gather.23.cloned.1.call-update) | async-done | bytes 33554448 | tf_op jit(solution)/shard_map/all_gather | solution.py:106
  1036.7 21.5 fusion.99
  1058.3 17.5 fusion.45
  1093.2 7.3 convolution_convert_fusion.4
  1111.4 6.3 multiply_reduce_fusion
  1129.2 20.3 collective-permute-done.3
  1152.0 29.3 collective-permute-done.2
  1182.7 13.8 convolution_convert_fusion.2
  1196.6 18.4 convolution_convert_fusion
  1215.0 16.2 convolution_convert_fusion.1
  1234.7 44.1 %reduce-scatter.16.cloned.1.call-done = bf16[2048,256]{1,0:T(8,128)(2,1)} async-done(((bf16[2048,2048]{1,0:T(8,128)(2,1)}), bf16[2048,256]{1,0:T(8,128)(2,1)}) %reduce-scatter.16.cloned.1.call-update) | async-done | bytes 1048592 | tf_op jit(solution)/shard_map/reduce_scatter | solution.py:52
  1278.9 407.7 %reduce-scatter.12.cloned.1.call-done = bf16[256,3,2048]{2,0,1:T(8,128)(2,1)} async-done(((bf16[2048,3,2048]{2,0,1:T(8,128)(2,1)}), bf16[256,3,2048]{2,0,1:T(8,128)(2,1)}) %reduce-scatter.12.cloned.1.call-update) | async-done | bytes 3145744 | tf_op jit(solution)/shard_map/reduce_scatter | solution.py:49
  1686.7 546.5 %reduce-scatter.24.cloned.1.call-done = bf16[8192,256]{1,0:T(8,128)(2,1)} async-done(((bf16[8192,2048]{1,0:T(8,128)(2,1)}), bf16[8192,256]{1,0:T(8,128)(2,1)}) %reduce-scatter.24.cloned.1.call-update) | async-done | bytes 4194320 | tf_op jit(solution)/shard_map/reduce_scatter | solution.py:52
  2233.3 546.1 %reduce-scatter.20.cloned.1.call-done = bf16[256,8192]{1,0:T(8,128)(2,1)} async-done(((bf16[2048,8192]{1,0:T(8,128)(2,1)}), bf16[256,8192]{1,0:T(8,128)(2,1)}) %reduce-scatter.20.cloned.1.call-update) | async-done | bytes 4194320 | tf_op jit(solution)/shard_map/reduce_scatter | solution.py:49
  2782.4 11.5 all-reduce.11
  2793.9 19.7 fusion.29
  2815.9 11.9 fusion.36
  2829.0 38.6 %all-reduce.13 = (f32[2048]{0:T(1024)S(1)}, f32[2048]{0:T(1024)S(1)}, f32[2048]{0:T(1024)S(1)}, f32[2048]{0:T(1024)S(1)}, f32[2048]{0:T(1024)S(1)}, /*index=5*/f32[2048]{0:T(1024)S(1)}) all-reduce(f32[2048]{0:T(1024)S(1)} %get-tuple-element.16, f32[2048]{0:T(1024)S(1)} %reduce_sum.190, ...), channel_id=2, replica_groups=mesh['seq'=8,'batch'=4] {'seq','batch'}, use_global_device_ids=true, to_apply=%region_12.13.clone | all-reduce | flops 12288 | bytes 98304
  2876.1 21.3 all-reduce.15
  2902.9 16.1 reduce-scatter.26.cloned.1.call-done
  2921.7 44.4 %reduce-scatter.22.cloned.1.call-done = bf16[256,2048]{1,0:T(8,128)(2,1)} async-done(((bf16[256,8192]{1,0:T(8,128)(2,1)}), bf16[256,2048]{1,0:T(8,128)(2,1)}) %reduce-scatter.22.cloned.1.call-update) | async-done | bytes 1048592 | tf_op jit(solution)/shard_map/reduce_scatter | solution.py:175
  (214 shorter events, 140.7 us)
Async XLA Ops:
  7.2 455.7 %copy-start = (s32[4,1]{0,1:T(1,128)S(1)}, s32[4,1]{0,1:T(1,128)}, u32[]{:S(2)}) copy-start(s32[4,1]{0,1:T(1,128)} %param.16) | copy-start | bytes 52
  7.2 106.1 %all-gather.9.cloned.1.call-start = ((), (), s32[]{:S(2)}) async-start(), calls=%async_computation.9 | async-start | bytes 7077888 | tf_op jit(solution)/shard_map/all_gather | solution.py:94
  9.6 155.1 %all-gather.13.cloned.1.call-start = ((), (), s32[]{:S(2)}) async-start(), calls=%async_computation.11 | async-start | bytes 2359296 | tf_op jit(solution)/shard_map/all_gather | solution.py:95
  10.3 279.6 %all-gather.17.cloned.1.call-start = ((), (), s32[]{:S(2)}) async-start(), calls=%async_computation.13 | async-start | bytes 9437184 | tf_op jit(solution)/shard_map/all_gather | solution.py:96
  11.0 404.4 %all-gather.21.cloned.1.call-start = ((), (), s32[]{:S(2)}) async-start(), calls=%async_computation.15 | async-start | bytes 9437184 | tf_op jit(solution)/shard_map/all_gather | solution.py:97
  11.6 559.2 %all-gather.11.cloned.1.call-start = ((), (), s32[]{:S(2)}) async-start(), calls=%async_computation.10 | async-start | bytes 31457280 | tf_op jit(solution)/shard_map/all_gather | solution.py:101
  113.3 538.0 %all-gather.15.cloned.1.call-start = ((), (), s32[]{:S(2)}) async-start(), calls=%async_computation.12 | async-start | bytes 10485760 | tf_op jit(solution)/shard_map/all_gather | solution.py:103
  164.7 669.0 %all-gather.19.cloned.1.call-start = ((), (), s32[]{:S(2)}) async-start(), calls=%async_computation.14 | async-start | bytes 41943040 | tf_op jit(solution)/shard_map/all_gather | solution.py:104
  290.0 746.8 %all-gather.23.cloned.1.call-start = ((), (), s32[]{:S(2)}) async-start(), calls=%async_computation.16 | async-start | bytes 41943040 | tf_op jit(solution)/shard_map/all_gather | solution.py:106
  415.5 41.2 %copy-start.24 = (bf16[2048]{0:T(1024)(128)(2,1)S(1)}, bf16[2048]{0:T(1024)(128)(2,1)}, u32[]{:S(2)}) copy-start(bf16[2048]{0:T(1024)(128)(2,1)} %param.27) | copy-start | bytes 12292
  415.5 47.9 %copy-start.26 = (bf16[2,512]{1,0:T(2,128)(2,1)S(1)}, bf16[2,512]{1,0:T(2,128)(2,1)}, u32[]{:S(2)}) copy-start(bf16[2,512]{1,0:T(2,128)(2,1)} %param.21) | copy-start | bytes 6148
  415.5 54.7 %copy-start.3 = (bf16[1,256,2048]{2,1,0:T(8,128)(2,1)S(1)}, bf16[1,256,2048]{2,1,0:T(8,128)(2,1)}, u32[]{:S(2)}) copy-start(bf16[1,256,2048]{2,1,0:T(8,128)(2,1)} %param.15) | copy-start | bytes 3145732
  415.5 863.3 %reduce-scatter.16.cloned.1.call-start = ((), (), s32[]{:S(2)}) async-start(), calls=%async_computation.19 | async-start | bytes 9437184 | tf_op jit(solution)/shard_map/reduce_scatter | solution.py:52
  470.8 113.9 %copy-start.22 = (f32[256]{0:T(256)}, f32[256]{0:T(256)S(1)}, u32[]{:S(2)}) copy-start(f32[256]{0:T(256)S(1)} %fusion.35) | copy-start | bytes 3076
  587.6 27.4 collective-permute-start
  595.1 41.7 %collective-permute-start.1 = (bf16[1,256,2048]{2,1,0:T(8,128)(2,1)}, bf16[1,256,2048]{2,1,0:T(8,128)(2,1)}, u32[]{:S(2)}, u32[]{:S(2)}) collective-permute-start(bf16[1,256,2048]{2,1,0:T(8,128)(2,1)} %get-tuple-element.39), channel_id=1, source_target_pairs={{0,4},{4,8},{8,12},{12,16},{16,20},{20,24},{24,28},{1,5},{5,9},{9,... | collective-permute-start | bytes 3145736 | tf_op jit(solution)/shard_map/ppermute | solution.py:13
  605.6 32.8 %copy-start.6 = (f32[1,256,1,2048]{1,3,2,0:T(8,128)}, f32[1,256,1,2048]{1,3,2,0:T(8,128)S(1)}, u32[]{:S(2)}) copy-start(f32[1,256,1,2048]{1,3,2,0:T(8,128)S(1)} %copy.72) | copy-start | bytes 6291460
  1086.6 600.1 %reduce-scatter.12.cloned.1.call-start = ((), (), s32[]{:S(2)}) async-start(), calls=%async_computation.17 | async-start | bytes 28311552 | tf_op jit(solution)/shard_map/reduce_scatter | solution.py:49
  1108.6 40.9 %copy-start.4 = (f32[16,128,512]{2,1,0:T(8,128)}, f32[16,128,512]{2,1,0:T(8,128)S(1)}, u32[]{:S(2)}) copy-start(f32[16,128,512]{2,1,0:T(8,128)S(1)} %fusion.11) | copy-start | bytes 12582916
  1109.8 39.7 %collective-permute-start.3 = (bf16[1,256,2048]{1,2,0:T(8,128)(2,1)}, bf16[1,256,2048]{1,2,0:T(8,128)(2,1)}, u32[]{:S(2)}, u32[]{:S(2)}) collective-permute-start(bf16[1,256,2048]{1,2,0:T(8,128)(2,1)} %slice.68), channel_id=1, source_target_pairs={{4,0},{8,4},{12,8},{16,12},{20,16},{24,20},{28,24},{5,1},{9,5},{13... | collective-permute-start | bytes 3145736 | tf_op jit(solution)/shard_map/ppermute | solution.py:13
  1125.3 56.0 %collective-permute-start.2 = (bf16[1,256,2048]{1,2,0:T(8,128)(2,1)S(1)}, bf16[1,256,2048]{1,2,0:T(8,128)(2,1)S(1)}, u32[]{:S(2)}, u32[]{:S(2)}) collective-permute-start(bf16[1,256,2048]{1,2,0:T(8,128)(2,1)S(1)} %slice.69), channel_id=1, source_target_pairs={{4,0},{8,4},{12,8},{16,12},{20,16},{24,20},{28,24},{5,1},{9,5},{13... | collective-permute-start | bytes 3145736 | tf_op jit(solution)/shard_map/ppermute | solution.py:13
  1196.5 1036.7 %reduce-scatter.24.cloned.1.call-start = ((), (), s32[]{:S(2)}) async-start(), calls=%async_computation.23 | async-start | bytes 37748736 | tf_op jit(solution)/shard_map/reduce_scatter | solution.py:52
  1215.0 1564.5 %reduce-scatter.20.cloned.1.call-start = ((), (), s32[]{:S(2)}) async-start(), calls=%async_computation.21 | async-start | bytes 37748736 | tf_op jit(solution)/shard_map/reduce_scatter | solution.py:49
  1231.2 1643.9 %reduce-scatter.28.cloned.1.call-start = ((), (), s32[]{:S(2)}) async-start(), calls=%async_computation.25 | async-start | bytes 655360
  1234.7 1663.9 %reduce-scatter.18.cloned.1.call-start = ((), (), s32[]{:S(2)}) async-start(), calls=%async_computation.20 | async-start | bytes 1310720 | tf_op jit(solution)/shard_map/reduce_scatter | solution.py:252
  1278.9 1621.5 %reduce-scatter.14.cloned.1.call-start = ((), (), s32[]{:S(2)}) async-start(), calls=%async_computation.18 | async-start | bytes 3932160 | tf_op jit(solution)/shard_map/reduce_scatter | solution.py:246
  1686.7 1232.3 %reduce-scatter.26.cloned.1.call-start = ((), (), s32[]{:S(2)}) async-start(), calls=%async_computation.24 | async-start | bytes 5242880 | tf_op jit(solution)/shard_map/reduce_scatter | solution.py:181
  2233.3 546.2 %copy-start.33 = (u32[32]{0:T(128)S(1)}, u32[32]{0:T(128)}, u32[]{:S(2)}) copy-start(u32[32]{0:T(128)} %constant.159) | copy-start | bytes 388
  2233.3 546.8 %copy-start.25 = (bf16[2048]{0:T(1024)(128)(2,1)S(1)}, bf16[2048]{0:T(1024)(128)(2,1)}, u32[]{:S(2)}) copy-start(bf16[2048]{0:T(1024)(128)(2,1)} %get-tuple-element.27) | copy-start | bytes 12292
  2233.3 732.8 %reduce-scatter.22.cloned.1.call-start = ((), (), s32[]{:S(2)}) async-start(), calls=%async_computation.22 | async-start | bytes 5242880 | tf_op jit(solution)/shard_map/reduce_scatter | solution.py:175
  2793.9 19.7 copy-start.21
  2900.4 68.5 %copy-start.1 = (s32[4,1]{0,1:T(1,128)S(1)}, s32[4,1]{0,1:T(1,128)}, u32[]{:S(2)}) copy-start(s32[4,1]{0,1:T(1,128)} %param.16) | copy-start | bytes 52
  (26 other events, 127.4 us)
Sparse Core Ops, SparseCore 0:
  10.6 102.6 all-gather.8
  115.4 49.2 all-gather.12
  166.8 123.1 all-gather.16
  291.8 123.5 all-gather.20
  416.9 153.9 all-gather.10
  572.2 58.2 all-gather.14
  632.1 201.5 all-gather.18
  835.2 201.4 all-gather.22
  1086.7 192.1 reduce-scatter.15
  1283.1 403.4 reduce-scatter.11
  1690.9 542.2 reduce-scatter.23
  2237.3 542.0 reduce-scatter.19
  2782.7 20.7 reduce-scatter.27
  2805.9 24.8 reduce-scatter.17
  2833.3 38.6 reduce-scatter.13
  2874.4 44.4 reduce-scatter.25
  2921.5 44.5 reduce-scatter.21
where the time goes:
time: 2980 us
  waiting for transfers between devices  2540 us (85%)
  matrix products  202 us (7%)
  blocking collectives  122 us (4%)
  other arithmetic  46 us (2%)
  local copies, waits for them, and re-layouts  41 us (1%)
    reduce_scatter x2, waiting for transfers between devices, rows_total(): lax.psum_scatter(pair[0].astype(jnp.bfloat16), 'seq', scatter_dimension=0...  954 us
    reduce_scatter x2, waiting for transfers between devices, rows_total(): lax.psum_scatter(pair[1].astype(jnp.bfloat16), 'seq', scatter_dimension=1...  591 us
    all_gather x1, waiting for transfers between devices, shards(): lax.all_gather(proj_down, 'batch', axis=0, tiled=True)  181 us
    all_gather x1, waiting for transfers between devices, shards(): lax.all_gather(proj_up, 'batch', axis=1, tiled=True)  173 us
    all_gather x1, waiting for transfers between devices, shards(): lax.all_gather(w_proj, 'seq', axis=1, tiled=True)  125 us
    all_gather x1, waiting for transfers between devices, shards(): lax.all_gather(w_fc, 'seq', axis=0, tiled=True)  125 us
    all_gather x1, waiting for transfers between devices, shards(): lax.all_gather(w_qkv, 'seq', axis=0, tiled=True)  102 us
    all_gather x1, waiting for transfers between devices, shards(): lax.all_gather(proj_in, 'batch', axis=2, tiled=True)  99.9 us
  transfers between devices with their start and end apart: 21, of which 17 were waited for; matrix products, arithmetic and copies ran while one was open for 8% of the time, Pallas kernels for 0%

commit v1 on v0

--- a/solution.py
+++ b/solution.py
@@ -5,6 +5,27 @@
 
 HEAD_DIM = 128
 WINDOW = 256
+
+
+def collect(array, axis, dim):
+    peers, index, width = (lax.axis_size(axis), lax.axis_index(axis), array.shape[dim])
+    right = [(i, (i + 1) % peers) for i in range(peers)]
+    downward = [(i, (i - 1) % peers) for i in range(peers)]
+    whole = jnp.zeros((*array.shape[:dim], peers * width, *array.shape[dim + 1 :]), array.dtype)
+    whole = lax.dynamic_update_slice_in_dim(whole, array, index * width, axis=dim)
+    from_left = from_right = array
+    halfway = peers // 2
+    for turn in range(1, halfway + 1):
+        from_left = lax.ppermute(from_left, axis, right)
+        whole = lax.dynamic_update_slice_in_dim(
+            whole, from_left, (index - turn) % peers * width, axis=dim
+        )
+        if turn < peers - halfway:
+            from_right = lax.ppermute(from_right, axis, downward)
+            whole = lax.dynamic_update_slice_in_dim(
+                whole, from_right, (index + turn) % peers * width, axis=dim
+            )
+    return whole
 
 
 def shifted(value, axis, steps):
@@ -103,7 +124,7 @@
         lax.all_gather(proj_mix, "batch", axis=0, tiled=True),
         lax.all_gather(proj_up, "batch", axis=1, tiled=True),
         lax.all_gather(fc_bias, "batch", axis=0, tiled=True),
-        lax.all_gather(proj_down, "batch", axis=0, tiled=True),
+        collect(proj_down, "batch", 0),
     )
     local_width = proj_in.shape[2]
     local_heads = local_width // head_dim

time: 2980 us -> 3120 us (1.047)
  blocking collectives: 122 us -> 344 us
  waiting for transfers between devices: 2540 us -> 2400 us
  local copies, waits for them, and re-layouts: 41 us -> 85.8 us
    ppermute x0 -> x3, waiting for transfers between devices: none -> 328 us  [the longest x2 328 us: collect(): from_left = lax.ppermute(from_left, axis, right)]
    unnamed x3, blocking collectives: 89.2 us -> 311 us
    all_gather x1 -> x0, waiting for transfers between devices: 181 us -> none  [shards(): lax.all_gather(proj_down, 'batch', axis=0, tiled=True)]
    all_gather x1, waiting for transfers between devices: 173 us -> 0.02 us  [shards(): lax.all_gather(proj_up, 'batch', axis=1, tiled=True)]
    all_gather x1, waiting for transfers between devices: 99.9 us -> 0.01 us  [shards(): lax.all_gather(proj_in, 'batch', axis=2, tiled=True)]
    dynamic_update_slice x0 -> x4, local copies, waits for them, and re-layouts: none -> 33.2 us  [the longest x2 16.6 us: collect(): lax.dynamic_update_slice_in_dim(whole, from_left, (index - turn) % peers...]
  transfers between devices with their start and end apart: 21 -> 23, of which waited for: 17 -> 14; matrix products, arithmetic and copies ran while one was open for 8% -> 8% of each run, Pallas kernels for 0% -> 0%
where the time goes in v1:
time: 3120 us; the launch traced here: 3110 us
  waiting for transfers between devices  2400 us (77%)
  blocking collectives  344 us (11%)
  matrix products  194 us (6%)
  local copies, waits for them, and re-layouts  85.8 us (3%)
  other arithmetic  45.9 us (1%)
    reduce_scatter x2, waiting for transfers between devices, rows_total(): lax.psum_scatter(pair[0].astype(jnp.bfloat16), 'seq', scatter_dimension=0...  954 us
    reduce_scatter x2, waiting for transfers between devices, rows_total(): lax.psum_scatter(pair[1].astype(jnp.bfloat16), 'seq', scatter_dimension=1...  594 us
    ppermute x2, waiting for transfers between devices, collect(): from_left = lax.ppermute(from_left, axis, right)  328 us
    unnamed x3, blocking collectives  311 us
    all_gather x1, waiting for transfers between devices, shards(): lax.all_gather(w_proj, 'seq', axis=1, tiled=True)  125 us
    all_gather x1, waiting for transfers between devices, shards(): lax.all_gather(w_fc, 'seq', axis=0, tiled=True)  125 us
    all_gather x1, waiting for transfers between devices, shards(): lax.all_gather(w_qkv, 'seq', axis=0, tiled=True)  102 us
    ppermute x4, waiting for transfers between devices, shifted(): lax.ppermute(value, axis, [(source, source + steps) for source in range(i...  63 us
  transfers between devices with their start and end apart: 23, of which 14 were waited for; matrix products, arithmetic and copies ran while one was open for 8% of the time, Pallas kernels for 0%

profile of v1, /device:TPU:0, one launch (start us, length us, event | category | flops | bytes accessed | tf_op | source)
XLA Modules:
  0.0 3106.0 jit_solution(245834061463324512)
XLA Ops:
  11.7 101.7 %all-gather.8.cloned.1.call-done = bf16[2048,3,512]{0,2,1:T(8,128)(2,1)} async-done(((bf16[256,3,512]{0,2,1:T(8,128)(2,1)}), bf16[2048,3,512]{0,2,1:T(8,128)(2,1)}) %all-gather.8.cloned.1.call-update) | async-done | bytes 6291472 | tf_op jit(solution)/shard_map/all_gather | solution.py:115
  113.4 51.3 %all-gather.12.cloned.1.call-done = bf16[512,2048]{1,0:T(8,128)(2,1)} async-done(((bf16[512,256]{1,0:T(8,128)(2,1)}), bf16[512,2048]{1,0:T(8,128)(2,1)}) %all-gather.12.cloned.1.call-update) | async-done | bytes 2097168 | tf_op jit(solution)/shard_map/all_gather | solution.py:116
  164.7 125.2 %all-gather.16.cloned.1.call-done = bf16[2048,2048]{1,0:T(8,128)(2,1)} async-done(((bf16[256,2048]{1,0:T(8,128)(2,1)}), bf16[2048,2048]{1,0:T(8,128)(2,1)}) %all-gather.16.cloned.1.call-update) | async-done | bytes 8388624 | tf_op jit(solution)/shard_map/all_gather | solution.py:117
  290.1 125.4 %all-gather.20.cloned.1.call-done = bf16[2048,2048]{1,0:T(8,128)(2,1)} async-done(((bf16[2048,256]{1,0:T(8,128)(2,1)}), bf16[2048,2048]{1,0:T(8,128)(2,1)}) %all-gather.20.cloned.1.call-update) | async-done | bytes 8388624 | tf_op jit(solution)/shard_map/all_gather | solution.py:118
  417.2 327.7 %collective-permute-done.2 = bf16[2048,2048]{1,0:T(8,128)(2,1)} collective-permute-done((bf16[2048,2048]{1,0:T(8,128)(2,1)}, bf16[2048,2048]{1,0:T(8,128)(2,1)}, u32[]{:S(2)}, u32[]{:S(2)}) %collective-permute-start.2) | collective-permute-done | bytes 8388640 | tf_op jit(solution)/shard_map/ppermute | solution.py:19
  748.7 261.2 %all-reduce.14 = (bf16[2048]{0:T(1024)(128)(2,1)S(1)}, bf16[2048]{0:T(1024)(128)(2,1)S(1)}, bf16[2048]{0:T(1024)(128)(2,1)S(1)}, bf16[2048]{0:T(1024)(128)(2,1)}...) all-reduce(bf16[2048]{0:T(1024)(128)(2,1)S(1)} %dynamic-update-slic, ...), channel_id=1, replica_groups=mesh['seq'=8,'batch'=4] {'seq','batch'}, use_global_device_ids=true, to_apply=%add.1 | all-reduce | flops 12288 | bytes 49152
  1024.6 11.1 broadcast_in_dim.48
  1035.7 8.3 constant_dynamic-update-slice_fusion.3
  1043.9 8.4 constant_dynamic-update-slice_fusion.2
  1052.3 8.4 constant_dynamic-update-slice_fusion.1
  1060.7 13.4 fusion.18
  1086.9 8.3 constant_dynamic-update-slice_fusion
  1110.6 15.7 collective-permute-done
  1148.4 17.3 convolution_add_fusion
  1165.6 21.5 fusion.99
  1187.1 17.5 fusion.45
  1258.1 21.1 collective-permute-done.6
  1281.9 26.1 collective-permute-done.5
  1309.4 13.8 convolution_convert_fusion.2
  1323.2 16.4 convolution_convert_fusion.1
  1339.7 18.2 convolution_convert_fusion
  1361.4 47.5 %reduce-scatter.16.cloned.1.call-done = bf16[2048,256]{1,0:T(8,128)(2,1)} async-done(((bf16[2048,2048]{1,0:T(8,128)(2,1)}), bf16[2048,256]{1,0:T(8,128)(2,1)}) %reduce-scatter.16.cloned.1.call-update) | async-done | bytes 1048592 | tf_op jit(solution)/shard_map/reduce_scatter | solution.py:73
  1409.0 407.8 %reduce-scatter.12.cloned.1.call-done = bf16[256,3,2048]{2,0,1:T(8,128)(2,1)} async-done(((bf16[2048,3,2048]{2,0,1:T(8,128)(2,1)}), bf16[256,3,2048]{2,0,1:T(8,128)(2,1)}) %reduce-scatter.12.cloned.1.call-update) | async-done | bytes 3145744 | tf_op jit(solution)/shard_map/reduce_scatter | solution.py:70
  1816.9 546.5 %reduce-scatter.20.cloned.1.call-done = bf16[256,8192]{1,0:T(8,128)(2,1)} async-done(((bf16[2048,8192]{1,0:T(8,128)(2,1)}), bf16[256,8192]{1,0:T(8,128)(2,1)}) %reduce-scatter.20.cloned.1.call-update) | async-done | bytes 4194320 | tf_op jit(solution)/shard_map/reduce_scatter | solution.py:70
  2363.4 546.2 %reduce-scatter.24.cloned.1.call-done = bf16[8192,256]{1,0:T(8,128)(2,1)} async-done(((bf16[8192,2048]{1,0:T(8,128)(2,1)}), bf16[8192,256]{1,0:T(8,128)(2,1)}) %reduce-scatter.24.cloned.1.call-update) | async-done | bytes 4194320 | tf_op jit(solution)/shard_map/reduce_scatter | solution.py:73
  2912.7 11.5 all-reduce.11
  2924.2 19.7 fusion.29
  2946.2 11.9 fusion.36
  2959.3 38.6 %all-reduce.13 = (f32[2048]{0:T(1024)S(1)}, f32[2048]{0:T(1024)S(1)}, f32[2048]{0:T(1024)S(1)}, f32[2048]{0:T(1024)S(1)}, f32[2048]{0:T(1024)S(1)}, /*index=5*/f32[2048]{0:T(1024)S(1)}) all-reduce(f32[2048]{0:T(1024)S(1)} %get-tuple-element.16, f32[2048]{0:T(1024)S(1)} %reduce_sum.190, ...), channel_id=2, replica_groups=mesh['seq'=8,'batch'=4] {'seq','batch'}, use_global_device_ids=true, to_apply=%region_12.13.clone | all-reduce | flops 12288 | bytes 98304
  3006.4 21.2 all-reduce.15
  3033.1 16.1 reduce-scatter.22.cloned.1.call-done
  3052.0 44.3 %reduce-scatter.26.cloned.1.call-done = bf16[2048,256]{1,0:T(8,128)(2,1)} async-done(((bf16[8192,256]{1,0:T(8,128)(2,1)}), bf16[2048,256]{1,0:T(8,128)(2,1)}) %reduce-scatter.26.cloned.1.call-update) | async-done | bytes 1048592 | tf_op jit(solution)/shard_map/reduce_scatter | solution.py:202
  (220 shorter events, 161.2 us)
Async XLA Ops:
  7.2 1009.0 %copy-start = (s32[4,1]{0,1:T(1,128)S(1)}, s32[4,1]{0,1:T(1,128)}, u32[]{:S(2)}) copy-start(s32[4,1]{0,1:T(1,128)} %param.16) | copy-start | bytes 52
  7.2 106.1 %all-gather.8.cloned.1.call-start = ((), (), s32[]{:S(2)}) async-start(), calls=%async_computation.9 | async-start | bytes 7077888 | tf_op jit(solution)/shard_map/all_gather | solution.py:115
  9.6 155.1 %all-gather.12.cloned.1.call-start = ((), (), s32[]{:S(2)}) async-start(), calls=%async_computation.11 | async-start | bytes 2359296 | tf_op jit(solution)/shard_map/all_gather | solution.py:116
  10.3 279.6 %all-gather.16.cloned.1.call-start = ((), (), s32[]{:S(2)}) async-start(), calls=%async_computation.13 | async-start | bytes 9437184 | tf_op jit(solution)/shard_map/all_gather | solution.py:117
  11.0 404.4 %all-gather.20.cloned.1.call-start = ((), (), s32[]{:S(2)}) async-start(), calls=%async_computation.15 | async-start | bytes 9437184 | tf_op jit(solution)/shard_map/all_gather | solution.py:118
  11.6 1049.0 %all-gather.10.cloned.1.call-start = ((), (), s32[]{:S(2)}) async-start(), calls=%async_computation.10 | async-start | bytes 31457280 | tf_op jit(solution)/shard_map/all_gather | solution.py:122
  113.3 1028.4 %all-gather.14.cloned.1.call-start = ((), (), s32[]{:S(2)}) async-start(), calls=%async_computation.12 | async-start | bytes 10485760 | tf_op jit(solution)/shard_map/all_gather | solution.py:124
  164.7 983.7 %all-gather.18.cloned.1.call-start = ((), (), s32[]{:S(2)}) async-start(), calls=%async_computation.14 | async-start | bytes 41943040 | tf_op jit(solution)/shard_map/all_gather | solution.py:125
  289.9 458.0 %copy-start.29 = (bf16[64]{0:T(256)(128)(2,1)S(1)}, bf16[64]{0:T(256)(128)(2,1)}, u32[]{:S(2)}) copy-start(bf16[64]{0:T(256)(128)(2,1)} %param.29) | copy-start | bytes 388
  289.9 458.3 %copy-start.30 = (bf16[64]{0:T(256)(128)(2,1)S(1)}, bf16[64]{0:T(256)(128)(2,1)}, u32[]{:S(2)}) copy-start(bf16[64]{0:T(256)(128)(2,1)} %param.25) | copy-start | bytes 388
  289.9 458.5 %copy-start.31 = (bf16[64]{0:T(256)(128)(2,1)S(1)}, bf16[64]{0:T(256)(128)(2,1)}, u32[]{:S(2)}) copy-start(bf16[64]{0:T(256)(128)(2,1)} %param.24) | copy-start | bytes 388
  290.0 720.0 %copy-start.23 = (bf16[2048]{0:T(1024)(128)(2,1)S(1)}, bf16[2048]{0:T(1024)(128)(2,1)}, u32[]{:S(2)}) copy-start(bf16[2048]{0:T(1024)(128)(2,1)} %param.27) | copy-start | bytes 12292
  290.0 726.8 %copy-start.25 = (bf16[2,512]{1,0:T(2,128)(2,1)S(1)}, bf16[2,512]{1,0:T(2,128)(2,1)}, u32[]{:S(2)}) copy-start(bf16[2,512]{1,0:T(2,128)(2,1)} %param.21) | copy-start | bytes 6148
  290.0 733.5 %copy-start.3 = (bf16[1,256,2048]{2,1,0:T(8,128)(2,1)S(1)}, bf16[1,256,2048]{2,1,0:T(8,128)(2,1)}, u32[]{:S(2)}) copy-start(bf16[1,256,2048]{2,1,0:T(8,128)(2,1)} %param.15) | copy-start | bytes 3145732
  290.0 1118.9 %reduce-scatter.16.cloned.1.call-start = ((), (), s32[]{:S(2)}) async-start(), calls=%async_computation.18 | async-start | bytes 9437184 | tf_op jit(solution)/shard_map/reduce_scatter | solution.py:73
  415.4 329.4 %collective-permute-start.2 = (bf16[2048,2048]{1,0:T(8,128)(2,1)}, bf16[2048,2048]{1,0:T(8,128)(2,1)}, u32[]{:S(2)}, u32[]{:S(2)}) collective-permute-start(bf16[2048,2048]{1,0:T(8,128)(2,1)} %all-gather.20.cloned.1.call-done), channel_id=1, source_target_pairs={{0,1},{1,2},{2,3},{3,0},{4,5},{5,6},{6,7},{7,4},{8,9},{9,10},{10,1... | collective-permute-start | bytes 25165832 | tf_op jit(solution)/shard_map/ppermute | solution.py:19
  415.4 636.9 %collective-permute-start.3 = (bf16[2048,2048]{1,0:T(8,128)(2,1)}, bf16[2048,2048]{1,0:T(8,128)(2,1)}, u32[]{:S(2)}, u32[]{:S(2)}) collective-permute-start(bf16[2048,2048]{1,0:T(8,128)(2,1)} %all-gather.20.cloned.1.call-done), channel_id=1, source_target_pairs={{0,3},{1,0},{2,1},{3,2},{4,7},{5,4},{6,5},{7,6},{8,11},{9,8},{10,9... | collective-permute-start | bytes 25165832 | tf_op jit(solution)/shard_map/ppermute | solution.py:24
  744.9 342.0 %collective-permute-start.4 = (bf16[2048,2048]{1,0:T(8,128)(2,1)}, bf16[2048,2048]{1,0:T(8,128)(2,1)}, u32[]{:S(2)}, u32[]{:S(2)}) collective-permute-start(bf16[2048,2048]{1,0:T(8,128)(2,1)} %collective-permute-done.2), channel_id=1, source_target_pairs={{0,1},{1,2},{2,3},{3,0},{4,5},{5,6},{6,7},{7,4},{8,9},{9,10},{10,1... | collective-permute-start | bytes 25165832 | tf_op jit(solution)/shard_map/ppermute | solution.py:19
  1076.9 51.7 %collective-permute-start.1 = (bf16[1,256,2048]{2,1,0:T(8,128)(2,1)}, bf16[1,256,2048]{2,1,0:T(8,128)(2,1)}, u32[]{:S(2)}, u32[]{:S(2)}) collective-permute-start(bf16[1,256,2048]{2,1,0:T(8,128)(2,1)} %get-tuple-element.39), channel_id=1, source_target_pairs={{0,4},{4,8},{8,12},{12,16},{16,20},{20,24},{24,28},{1,5},{5,9},{9,... | collective-permute-start | bytes 3145736 | tf_op jit(solution)/shard_map/ppermute | solution.py:34
  1084.4 41.9 %collective-permute-start = (bf16[1,256,2048]{2,1,0:T(8,128)(2,1)}, bf16[1,256,2048]{2,1,0:T(8,128)(2,1)}, u32[]{:S(2)}, u32[]{:S(2)}) collective-permute-start(bf16[1,256,2048]{2,1,0:T(8,128)(2,1)} %fusion.47), channel_id=1, source_target_pairs={{0,4},{4,8},{8,12},{12,16},{16,20},{20,24},{24,28},{1,5},{5,9},{9,... | collective-permute-start | bytes 3145736 | tf_op jit(solution)/shard_map/ppermute | solution.py:34
  1215.5 601.3 %reduce-scatter.12.cloned.1.call-start = ((), (), s32[]{:S(2)}) async-start(), calls=%async_computation.16 | async-start | bytes 28311552 | tf_op jit(solution)/shard_map/reduce_scatter | solution.py:70
  1238.9 40.4 %collective-permute-start.6 = (bf16[1,256,2048]{1,2,0:T(8,128)(2,1)}, bf16[1,256,2048]{1,2,0:T(8,128)(2,1)}, u32[]{:S(2)}, u32[]{:S(2)}) collective-permute-start(bf16[1,256,2048]{1,2,0:T(8,128)(2,1)} %slice.68), channel_id=1, source_target_pairs={{4,0},{8,4},{12,8},{16,12},{20,16},{24,20},{28,24},{5,1},{9,5},{13... | collective-permute-start | bytes 3145736 | tf_op jit(solution)/shard_map/ppermute | solution.py:34
  1254.3 53.7 %collective-permute-start.5 = (bf16[1,256,2048]{1,2,0:T(8,128)(2,1)S(1)}, bf16[1,256,2048]{1,2,0:T(8,128)(2,1)S(1)}, u32[]{:S(2)}, u32[]{:S(2)}) collective-permute-start(bf16[1,256,2048]{1,2,0:T(8,128)(2,1)S(1)} %slice.69), channel_id=1, source_target_pairs={{4,0},{8,4},{12,8},{16,12},{20,16},{24,20},{28,24},{5,1},{9,5},{13... | collective-permute-start | bytes 3145736 | tf_op jit(solution)/shard_map/ppermute | solution.py:34
  1323.2 1040.2 %reduce-scatter.20.cloned.1.call-start = ((), (), s32[]{:S(2)}) async-start(), calls=%async_computation.20 | async-start | bytes 37748736 | tf_op jit(solution)/shard_map/reduce_scatter | solution.py:70
  1339.6 1570.0 %reduce-scatter.24.cloned.1.call-start = ((), (), s32[]{:S(2)}) async-start(), calls=%async_computation.22 | async-start | bytes 37748736 | tf_op jit(solution)/shard_map/reduce_scatter | solution.py:73
  1357.9 1647.5 %reduce-scatter.28.cloned.1.call-start = ((), (), s32[]{:S(2)}) async-start(), calls=%async_computation.24 | async-start | bytes 655360
  1361.4 1667.4 %reduce-scatter.18.cloned.1.call-start = ((), (), s32[]{:S(2)}) async-start(), calls=%async_computation.19 | async-start | bytes 1310720 | tf_op jit(solution)/shard_map/reduce_scatter | solution.py:273
  1409.0 1621.6 %reduce-scatter.14.cloned.1.call-start = ((), (), s32[]{:S(2)}) async-start(), calls=%async_computation.17 | async-start | bytes 3932160 | tf_op jit(solution)/shard_map/reduce_scatter | solution.py:267
  1816.8 1232.4 %reduce-scatter.22.cloned.1.call-start = ((), (), s32[]{:S(2)}) async-start(), calls=%async_computation.21 | async-start | bytes 5242880 | tf_op jit(solution)/shard_map/reduce_scatter | solution.py:196
  2363.4 546.4 %copy-start.24 = (bf16[2048]{0:T(1024)(128)(2,1)S(1)}, bf16[2048]{0:T(1024)(128)(2,1)}, u32[]{:S(2)}) copy-start(bf16[2048]{0:T(1024)(128)(2,1)} %get-tuple-element.27) | copy-start | bytes 12292
  2363.4 546.4 %copy-start.32 = (u32[32]{0:T(128)S(1)}, u32[32]{0:T(128)}, u32[]{:S(2)}) copy-start(u32[32]{0:T(128)} %constant.185) | copy-start | bytes 388
  2363.4 732.9 %reduce-scatter.26.cloned.1.call-start = ((), (), s32[]{:S(2)}) async-start(), calls=%async_computation.23 | async-start | bytes 5242880 | tf_op jit(solution)/shard_map/reduce_scatter | solution.py:202
  (27 other events, 1690.0 us)
Sparse Core Ops, SparseCore 0:
  10.6 102.6 all-gather.7
  115.4 49.2 all-gather.11
  166.8 123.1 all-gather.15
  291.8 123.5 all-gather.19
  416.9 287.9 all-gather.9
  706.3 88.5 all-gather.13
  796.4 255.8 all-gather.17
  1215.6 193.2 reduce-scatter.15
  1413.4 403.4 reduce-scatter.11
  1820.9 542.4 reduce-scatter.19
  2367.6 542.0 reduce-scatter.23
  2912.8 20.7 reduce-scatter.27
  2936.1 24.9 reduce-scatter.17
  2963.6 38.6 reduce-scatter.13
  3004.7 44.4 reduce-scatter.21
  3051.7 44.5 reduce-scatter.25
